TPU v7x, 256 devices: a whole 4x4x8 slice. The times are simulated.
256 devices in a mesh: dp: 2 (over x_lo), expert: 8 (over z), shard: 16 (over x_hi, y, core).
Axes of the slice: x: 4 (x_hi: 2, x_lo: 2; x = x_hi * 2 + x_lo), y: 4, z: 8, core: 2. Of those that a mesh axis runs over, the one named last changes fastest.
Arguments:
- tokens: bfloat16 [2048, 6144], P(('dp', 'expert', 'shard')), may hold values from -6 to 6
- gate_up_weight: bfloat16 [8, 2, 8192, 6144], P(None, None, ('dp', 'expert', 'shard')), may hold values from -0.078125 to 0.078125
- down_weight: bfloat16 [8, 8192, 6144], P(None, ('dp', 'expert', 'shard')), may hold values from -0.0625 to 0.0625
- expert_ids: int32 [2048, 2], P(('dp', 'expert', 'shard')), may hold values from 0 to 7, as said below
- slot_ids: int32 [2048, 2], P(('dp', 'expert', 'shard')), may hold values from 0 to 3, as said below
- gate_values: float32 [2048, 2], P(('dp', 'expert', 'shard')), may hold values from 0.1 to 1
- old_place: int32 [8], replicated, may hold values from 0 to 7, each once
- new_place: int32 [8], replicated, may hold values from 0 to 7, each once
Outputs:
- mixed_out: bfloat16 [2048, 6144], P(('dp', 'expert', 'shard'))
Inputs may be any that keep to these rules, and one draw needn't show every extreme that they name: `expert_ids`: each token names 2 different experts; among the 8 tokens of one block no expert is named more than 4 times, and one expert is named exactly 4 times in every block. `slot_ids`: within one block, two choices that name the same expert have different slots. `old_place`: each expert number appears once. `new_place`: each expert number appears once.
All inputs are finite; a program needn't handle non-finite values.
Results may differ from a plain program's by a relative error of at most 0.02.
Values may be sent and summed in bfloat16 or wider, within the bound.
A program may use at most 128 MiB of HBM per device.

v0:
```python
import jax
import jax.numpy as jnp
from jax import lax
from jax.sharding import PartitionSpec as P


def placement_order(old_place, new_place):
    slot_total = old_place.shape[0]
    matches = (new_place[:, None] == old_place[None, :]).astype(jnp.int32)
    return jnp.sum(matches * jnp.arange(slot_total, dtype=jnp.int32)[None, :], axis=1)


def swiglu_rows(row_block, pair_weight):
    gate_up = jnp.einsum("rd,gud->rgu", row_block, pair_weight, preferred_element_type=jnp.float32)
    return (jax.nn.silu(gate_up[:, 0]) * gate_up[:, 1]).astype(jnp.bfloat16)


def local(
    tokens, gate_up_weight, down_weight, expert_ids, slot_ids, gate_values, old_place, new_place
):
    experts = gate_up_weight.shape[0]
    sliver = gate_up_weight.shape[2]
    model_width = tokens.shape[1]
    tok_rows = tokens.shape[0]
    choices_per_token = expert_ids.shape[1]
    capacity = 2 * tok_rows * choices_per_token // experts
    cell_count = experts * capacity
    data_ways = lax.axis_size("dp")
    slot_order = placement_order(old_place, new_place)
    cell_ids = expert_ids * capacity + slot_ids
    cell_range = jnp.arange(cell_count, dtype=jnp.int32)
    cell_hits = (cell_ids[:, :, None] == cell_range[None, None, :]).astype(jnp.float32)
    token_picks = jnp.sum(cell_hits, axis=1)
    dispatched = jnp.dot(
        token_picks.T.astype(jnp.bfloat16), tokens, preferred_element_type=jnp.float32
    ).astype(jnp.bfloat16)
    received = lax.all_to_all(
        dispatched.reshape(experts, capacity, model_width),
        "expert",
        split_axis=0,
        concat_axis=0,
        tiled=True,
    )
    own_rows = received.reshape(cell_count, model_width)
    sectioned_in = gate_up_weight.reshape(experts, 2, data_ways, sliver // data_ways, model_width)
    sectioned_down = down_weight.reshape(experts, 1, data_ways, sliver // data_ways, model_width)
    sectioned_in = jnp.take(sectioned_in, slot_order, axis=0)
    sectioned_down = jnp.take(sectioned_down, slot_order, axis=0)
    relaid_in, relaid_down = (
        lax.all_to_all(
            lax.all_to_all(sectioned_in, "dp", split_axis=2, concat_axis=3, tiled=True),
            "expert",
            split_axis=0,
            concat_axis=3,
            tiled=True,
        ),
        lax.all_to_all(
            lax.all_to_all(sectioned_down, "dp", split_axis=2, concat_axis=3, tiled=True),
            "expert",
            split_axis=0,
            concat_axis=3,
            tiled=True,
        ),
    )
    full_in, full_down = (
        lax.all_gather(relaid_in, "dp", axis=3, tiled=True),
        lax.all_gather(relaid_down, "dp", axis=3, tiled=True),
    )
    pair_in = full_in.reshape(2, -1, model_width)
    pair_down = full_down.reshape(-1, model_width)
    group_rows = lax.all_gather(own_rows, "shard", axis=0, tiled=True)
    summed = lax.psum_scatter(
        jnp.dot(
            swiglu_rows(group_rows, pair_in), pair_down, preferred_element_type=jnp.float32
        ).astype(jnp.bfloat16),
        "shard",
        scatter_dimension=0,
        tiled=True,
    )
    returned = lax.all_to_all(
        summed.reshape(experts, capacity, model_width),
        "expert",
        split_axis=0,
        concat_axis=0,
        tiled=True,
    )
    combine_weights = jnp.sum(cell_hits * gate_values[:, :, None], axis=1)
    mixed_out = jnp.dot(
        combine_weights,
        returned.reshape(cell_count, model_width).astype(jnp.float32),
        precision=lax.Precision.HIGHEST,
    )
    return mixed_out.astype(jnp.bfloat16)


def solution(mesh):
    in_specs = (
        P(("dp", "expert", "shard"), None),
        P(None, None, ("dp", "expert", "shard"), None),
        P(None, ("dp", "expert", "shard"), None),
        P(("dp", "expert", "shard"), None),
        P(("dp", "expert", "shard"), None),
        P(("dp", "expert", "shard"), None),
        P(),
        P(),
    )
    out_specs = P(("dp", "expert", "shard"), None)
    return jax.shard_map(local, mesh=mesh, in_specs=in_specs, out_specs=out_specs, check_vma=False)
```

profile of v0, /device:TPU:8, one launch (start us, length us, event | category | flops | bytes accessed | tf_op | source)
XLA Modules:
  0.0 681.6 jit_solution(10519561180992360223)
XLA Ops:
  8.3 1.2 convolution_convert_fusion.1
  9.5 0.9 reshape.64
  10.4 8.5 %all-to-all-start = ((bf16[8,4,6144]{2,1,0:T(4,128)(2,1)}), bf16[8,4,6144]{2,1,0:T(4,128)(2,1)S(1)}, u32[]{:S(2)}, u32[]{:S(2)}) async-start(bf16[8,4,6144]{2,1,0:T(4,128)(2,1)} %reshape.64), calls=%async_computation | async-start | bytes 786432 | tf_op jit(solution)/shard_map/all_to_all | solution.py:37
  19.7 6.4 gather_fusion
  26.1 3.5 broadcast_select_fusion
  29.6 3.1 copy.24
  33.5 6.3 all-to-all-start.1
  40.8 89.5 %all-to-all-done.1 = bf16[8,2,2,16,6144]{4,3,1,0,2:T(8,128)(2,1)} async-done(((bf16[8,2,2,16,6144]{4,3,1,0,2:T(8,128)(2,1)}), bf16[8,2,2,16,6144]{4,3,1,0,2:T(8,128)(2,1)}, u32[]{:S(2)}, u32[]{:S(2)}) %all-to-all-start.1) | async-done | bytes 6291488 | tf_op jit(solution)/shard_map/all_to_all | solution.py:51
  130.3 3.5 copy.25
  133.8 145.8 %all_to_all.64 = bf16[8,2,1,32,6144]{4,3,1,2,0:T(8,128)(2,1)S(1)} all-to-all(bf16[8,2,1,32,6144]{4,3,1,2,0:T(8,128)(2,1)S(1)} %bitcast.37), channel_id=1, replica_groups=mesh['dp'=2,'expert'=8,'shard'=16] {'expert'}, dimensions={0} | all-to-all | bytes 12582912 | tf_op jit(solution)/shard_map/all_to_all | solution.py:50
  279.7 3.1 copy.27
  282.8 2.4 gather_fusion.1
  285.3 2.3 bitcast_select_fusion
  287.9 63.1 %all_to_all.65 = bf16[8,1,2,16,6144]{4,3,0,1,2:T(8,128)(2,1)S(1)} all-to-all(bf16[8,1,2,16,6144]{4,3,0,1,2:T(8,128)(2,1)S(1)} %copy.28), channel_id=1, replica_groups=mesh['dp'=2,'expert'=8,'shard'=16] {'dp'}, dimensions={2} | all-to-all | bytes 6291456 | tf_op jit(solution)/shard_map/all_to_all | solution.py:58
  351.2 66.1 %all_to_all.66 = bf16[8,1,1,32,6144]{4,3,2,1,0:T(8,128)(2,1)} all-to-all(bf16[8,1,1,32,6144]{4,3,2,1,0:T(8,128)(2,1)S(1)} %bitcast.40), channel_id=1, replica_groups=mesh['dp'=2,'expert'=8,'shard'=16] {'expert'}, dimensions={0} | all-to-all | bytes 6291456 | tf_op jit(solution)/shard_map/all_to_all | solution.py:57
  417.5 41.2 %all-gather.6.cloned.1.call-done = bf16[1,2,1,512,6144]{4,3,1,2,0:T(8,128)(2,1)} async-done(((bf16[1,2,1,256,6144]{4,3,1,2,0:T(8,128)(2,1)}), bf16[1,2,1,512,6144]{4,3,1,2,0:T(8,128)(2,1)}) %all-gather.6.cloned.1.call-update) | async-done | bytes 12582928 | tf_op jit(solution)/shard_map/all_gather | solution.py:66
  458.6 12.5 %fusion = f32[512,2,512]{2,0,1:T(8,128)} fusion(bf16[1,2,1,512,6144]{4,3,1,2,0:T(8,128)(2,1)} %all-gather.6.cloned.1.call-done, bf16[512,6144]{1,0:T(8,128)(2,1)} %all-gather.4.cloned.1.call-done), kind=kOutput, calls=%fused_computation.2 | convolution fusion | flops 6442450944 | bytes 20971520 | tf_op jit(solution)/shard_map/rd,gud->rgu/dot_general | solution.py:14
  471.2 72.6 %all-gather.8.cloned.1.call-done = bf16[1,1,1,512,6144]{4,3,2,1,0:T(8,128)(2,1)} async-done(((bf16[1,1,1,256,6144]{4,3,2,1,0:T(8,128)(2,1)}), bf16[1,1,1,512,6144]{4,3,2,1,0:T(8,128)(2,1)}) %all-gather.8.cloned.1.call-update) | async-done | bytes 6291472 | tf_op jit(solution)/shard_map/all_gather | solution.py:67
  543.8 9.7 %convolution_convert_fusion = bf16[512,6144]{1,0:T(8,128)(2,1)} fusion(bf16[1,1,1,512,6144]{4,3,2,1,0:T(8,128)(2,1)} %all-gather.8.cloned.1.call-done, f32[512,2,512]{2,0,1:T(8,128)} %fusion), kind=kOutput, calls=%fused_computation.4 | convolution fusion | flops 3225944064 | bytes 14680064 | tf_op jit(solution)/shard_map/dot_general | solution.py:73
  553.6 98.3 %reduce-scatter.2.cloned.1.call-done = bf16[32,6144]{1,0:T(8,128)(2,1)} async-done(((bf16[512,6144]{1,0:T(8,128)(2,1)}), bf16[32,6144]{1,0:T(8,128)(2,1)}) %reduce-scatter.2.cloned.1.call-update) | async-done | bytes 393232 | tf_op jit(solution)/shard_map/reduce_scatter | solution.py:72
  651.9 1.1 reshape.70
  653.0 20.0 %all_to_all.67 = bf16[8,4,6144]{2,1,0:T(4,128)(2,1)} all-to-all(bf16[8,4,6144]{2,1,0:T(4,128)(2,1)S(1)} %reshape.70), channel_id=1, replica_groups=mesh['dp'=2,'expert'=8,'shard'=16] {'expert'}, dimensions={0} | all-to-all | bytes 786432 | tf_op jit(solution)/shard_map/all_to_all | solution.py:80
  673.1 1.1 reshape.71
  674.1 0.9 convolution_convert_fusion.2
  (23 shorter events, 5.2 us)
Async XLA Ops:
  6.5 276.3 %copy-start = (bf16[8,32,6144]{2,1,0:T(8,128)(2,1)S(1)}, bf16[8,32,6144]{2,1,0:T(8,128)(2,1)}, u32[]{:S(2)}) copy-start(bf16[8,32,6144]{2,1,0:T(8,128)(2,1)} %param.10) | copy-start | bytes 9437188
  10.4 23.2 %all-to-all-start = ((bf16[8,4,6144]{2,1,0:T(4,128)(2,1)}), bf16[8,4,6144]{2,1,0:T(4,128)(2,1)S(1)}, u32[]{:S(2)}, u32[]{:S(2)}) async-start(bf16[8,4,6144]{2,1,0:T(4,128)(2,1)} %reshape.64), calls=%async_computation | async-start | bytes 786432 | tf_op jit(solution)/shard_map/all_to_all | solution.py:37
  33.5 96.8 %all-to-all-start.1 = ((bf16[8,2,2,16,6144]{4,3,1,0,2:T(8,128)(2,1)}), bf16[8,2,2,16,6144]{4,3,1,0,2:T(8,128)(2,1)}, u32[]{:S(2)}, u32[]{:S(2)}) async-start(bf16[8,2,2,16,6144]{4,3,1,0,2:T(8,128)(2,1)} %copy.24), calls=%async_computation.1 | async-start | bytes 12582912 | tf_op jit(solution)/shard_map/all_to_all | solution.py:51
  39.8 377.6 %all-gather.4.cloned.1.call-start = ((), (), s32[]{:S(2)}) async-start(), calls=%async_computation.7 | async-start | bytes 6684672 | tf_op jit(solution)/shard_map/all_gather | solution.py:71
  40.8 417.9 %all-gather.6.cloned.1.call-start = ((), (), s32[]{:S(2)}) async-start(), calls=%async_computation.8 | async-start | bytes 18874368 | tf_op jit(solution)/shard_map/all_gather | solution.py:66
  282.8 261.0 %all-gather.8.cloned.1.call-start = ((), (), s32[]{:S(2)}) async-start(), calls=%async_computation.9 | async-start | bytes 9437184 | tf_op jit(solution)/shard_map/all_gather | solution.py:67
  417.4 234.5 %reduce-scatter.2.cloned.1.call-start = ((), (), s32[]{:S(2)}) async-start(), calls=%async_computation.10 | async-start | bytes 6684672 | tf_op jit(solution)/shard_map/reduce_scatter | solution.py:72
  543.8 131.2 %copy-start.1 = (bf16[8,32,6144]{2,1,0:T(8,128)(2,1)S(1)}, bf16[8,32,6144]{2,1,0:T(8,128)(2,1)}, u32[]{:S(2)}) copy-start(bf16[8,32,6144]{2,1,0:T(8,128)(2,1)} %param.10) | copy-start | bytes 9437188
Sparse Core Ops, SparseCore 0:
  43.4 90.1 all-gather.3
  282.9 175.6 all-gather.5
  460.4 83.3 all-gather.7
  553.7 98.1 reduce-scatter.1
where the time goes:
time: 682 us
  waiting for transfers between devices  303 us (44%)
  blocking collectives  295 us (43%)
  matrix products  24.3 us (4%)
  local copies, waits for them, and re-layouts  23.1 us (3%)
  starting transfers between devices  15 us (2%)
  between operations  13.2 us (2%)
  other arithmetic  8.31 us (1%)
    all_to_all x1, blocking collectives, local(): lax.all_to_all(lax.all_to_all(sectioned_in, 'dp', split_axis=2, concat_ax...  146 us
    reduce_scatter x1, waiting for transfers between devices, local(): lax.psum_scatter(jnp.dot(swiglu_rows(group_rows, pair_in), pair_down, pre...  98.3 us
    all_to_all x1, waiting for transfers between devices, local(): lax.all_to_all(sectioned_in, 'dp', split_axis=2, concat_axis=3, tiled=True)  89.5 us
    all_gather x1, waiting for transfers between devices, local(): lax.all_gather(relaid_down, 'dp', axis=3, tiled=True)  72.6 us
    all_to_all x1, blocking collectives, local(): lax.all_to_all(lax.all_to_all(sectioned_down, 'dp', split_axis=2, concat_...  66.1 us
    all_to_all x1, blocking collectives, local(): lax.all_to_all(sectioned_down, 'dp', split_axis=2, concat_axis=3, tiled=T...  63.1 us
    all_gather x1, waiting for transfers between devices, local(): lax.all_gather(relaid_in, 'dp', axis=3, tiled=True)  41.2 us
    all_to_all x1, blocking collectives, local(): lax.all_to_all(summed.reshape(experts, capacity, model_width), 'expert',...  20 us
  transfers between devices with their start and end apart: 6, of which 5 were waited for; matrix products, arithmetic and copies ran while one was open for 6% of the time, Pallas kernels for 0%

commit v1 on v0

--- a/solution.py
+++ b/solution.py
@@ -64,7 +64,9 @@
     )
     full_in, full_down = (
         lax.all_gather(relaid_in, "dp", axis=3, tiled=True),
-        lax.all_gather(relaid_down, "dp", axis=3, tiled=True),
+        jnp.concatenate(
+            lax.all_to_all(jnp.stack([relaid_down] * lax.axis_size("dp")), "dp", 0, 0), axis=3
+        ),
     )
     pair_in = full_in.reshape(2, -1, model_width)
     pair_down = full_down.reshape(-1, model_width)

time: 682 us -> 661 us (0.969)
  waiting for transfers between devices: 303 us -> 272 us
    all_gather x1 -> x0, waiting for transfers between devices: 72.6 us -> none  [local(): lax.all_gather(relaid_down, 'dp', axis=3, tiled=True)]
    all_gather x1, waiting for transfers between devices: 41.2 us -> 68.2 us  [local(): lax.all_gather(relaid_in, 'dp', axis=3, tiled=True)]
    all_to_all x0 -> x1, waiting for transfers between devices: none -> 18.4 us  [local(): lax.all_to_all(jnp.stack([relaid_down] * lax.axis_size('dp')), 'dp', 0, 0)]
where the time goes in v1:
time: 661 us
  blocking collectives  295 us (45%)
  waiting for transfers between devices  272 us (41%)
  matrix products  24.3 us (4%)
  local copies, waits for them, and re-layouts  23.1 us (3%)
  starting transfers between devices  21.2 us (3%)
  between operations  13.2 us (2%)
  other arithmetic  11.5 us (2%)
    all_to_all x1, blocking collectives, local(): lax.all_to_all(lax.all_to_all(sectioned_in, 'dp', split_axis=2, concat_ax...  146 us
    reduce_scatter x1, waiting for transfers between devices, local(): lax.psum_scatter(jnp.dot(swiglu_rows(group_rows, pair_in), pair_down, pre...  95.3 us
    all_to_all x1, waiting for transfers between devices, local(): lax.all_to_all(sectioned_in, 'dp', split_axis=2, concat_axis=3, tiled=True)  89.5 us
    all_gather x1, waiting for transfers between devices, local(): lax.all_gather(relaid_in, 'dp', axis=3, tiled=True)  68.2 us
    all_to_all x1, blocking collectives, local(): lax.all_to_all(lax.all_to_all(sectioned_down, 'dp', split_axis=2, concat_...  66 us
    all_to_all x1, blocking collectives, local(): lax.all_to_all(sectioned_down, 'dp', split_axis=2, concat_axis=3, tiled=T...  63 us
    all_to_all x1, blocking collectives, local(): lax.all_to_all(summed.reshape(experts, capacity, model_width), 'expert',...  20 us
    all_to_all x1, waiting for transfers between devices, local(): lax.all_to_all(jnp.stack([relaid_down] * lax.axis_size('dp')), 'dp', 0, 0)  18.4 us
  transfers between devices with their start and end apart: 6, of which 5 were waited for; matrix products, arithmetic and copies ran while one was open for 6% of the time, Pallas kernels for 0%

profile of v1, /device:TPU:8, one launch (start us, length us, event | category | flops | bytes accessed | tf_op | source)
XLA Modules:
  0.0 660.6 jit_solution(4340669352122984994)
XLA Ops:
  8.3 1.2 convolution_convert_fusion.1
  10.4 8.5 %all-to-all-start = ((bf16[8,4,6144]{2,1,0:T(4,128)(2,1)}), bf16[8,4,6144]{2,1,0:T(4,128)(2,1)S(1)}, u32[]{:S(2)}, u32[]{:S(2)}) async-start(bf16[8,4,6144]{2,1,0:T(4,128)(2,1)} %reshape.62), calls=%async_computation | async-start | bytes 786432 | tf_op jit(solution)/shard_map/all_to_all | solution.py:37
  19.7 6.4 gather_fusion
  26.1 3.5 broadcast_select_fusion
  29.6 3.1 copy.24
  33.5 6.3 all-to-all-start.1
  40.8 89.5 %all-to-all-done.1 = bf16[8,2,2,16,6144]{4,3,1,0,2:T(8,128)(2,1)} async-done(((bf16[8,2,2,16,6144]{4,3,1,0,2:T(8,128)(2,1)}), bf16[8,2,2,16,6144]{4,3,1,0,2:T(8,128)(2,1)}, u32[]{:S(2)}, u32[]{:S(2)}) %all-to-all-start.1) | async-done | bytes 6291488 | tf_op jit(solution)/shard_map/all_to_all | solution.py:51
  130.3 3.5 copy.25
  133.8 145.9 %all_to_all.66 = bf16[8,2,1,32,6144]{4,3,1,2,0:T(8,128)(2,1)S(1)} all-to-all(bf16[8,2,1,32,6144]{4,3,1,2,0:T(8,128)(2,1)S(1)} %bitcast.36), channel_id=1, replica_groups=mesh['dp'=2,'expert'=8,'shard'=16] {'expert'}, dimensions={0} | all-to-all | bytes 12582912 | tf_op jit(solution)/shard_map/all_to_all | solution.py:50
  279.7 3.1 copy.27
  282.8 2.4 gather_fusion.1
  285.2 2.3 bitcast_select_fusion
  287.8 63.0 %all_to_all.67 = bf16[8,1,2,16,6144]{4,3,0,1,2:T(8,128)(2,1)S(1)} all-to-all(bf16[8,1,2,16,6144]{4,3,0,1,2:T(8,128)(2,1)S(1)} %copy.28), channel_id=1, replica_groups=mesh['dp'=2,'expert'=8,'shard'=16] {'dp'}, dimensions={2} | all-to-all | bytes 6291456 | tf_op jit(solution)/shard_map/all_to_all | solution.py:58
  351.2 66.0 %all_to_all.68 = bf16[8,1,1,32,6144]{4,3,2,1,0:T(8,128)(2,1)S(1)} all-to-all(bf16[8,1,1,32,6144]{4,3,2,1,0:T(8,128)(2,1)S(1)} %bitcast.38), channel_id=1, replica_groups=mesh['dp'=2,'expert'=8,'shard'=16] {'expert'}, dimensions={0} | all-to-all | bytes 6291456 | tf_op jit(solution)/shard_map/all_to_all | solution.py:57
  417.2 3.2 pad_maximum_fusion
  420.4 6.3 all-to-all-start.5
  426.8 68.2 %all-gather.5.cloned.1.call-done = bf16[1,2,1,512,6144]{4,3,1,2,0:T(8,128)(2,1)} async-done(((bf16[1,2,1,256,6144]{4,3,1,2,0:T(8,128)(2,1)}), bf16[1,2,1,512,6144]{4,3,1,2,0:T(8,128)(2,1)}) %all-gather.5.cloned.1.call-update) | async-done | bytes 12582928 | tf_op jit(solution)/shard_map/all_gather | solution.py:66
  495.0 12.5 %fusion = f32[512,2,512]{2,0,1:T(8,128)} fusion(bf16[1,2,1,512,6144]{4,3,1,2,0:T(8,128)(2,1)} %all-gather.5.cloned.1.call-done, bf16[512,6144]{1,0:T(8,128)(2,1)} %all-gather.3.cloned.1.call-done), kind=kOutput, calls=%fused_computation.2 | convolution fusion | flops 6442450944 | bytes 20971520 | tf_op jit(solution)/shard_map/rd,gud->rgu/dot_general | solution.py:14
  507.5 18.4 %all-to-all-done.5 = bf16[2,1,1,1,256,6144]{5,4,3,2,1,0:T(8,128)(2,1)} async-done(((bf16[2,1,1,1,256,6144]{5,4,3,2,1,0:T(8,128)(2,1)}), bf16[2,1,1,1,256,6144]{5,4,3,2,1,0:T(8,128)(2,1)}, u32[]{:S(2)}, u32[]{:S(2)}) %all-to-all-start.5) | async-done | bytes 6291488 | tf_op jit(solution)/shard_map/all_to_all | solution.py:68
  525.9 9.7 %convolution_convert_fusion = bf16[512,6144]{1,0:T(8,128)(2,1)} fusion(bf16[512,6144]{1,0:T(8,128)(2,1)} %bitcast.16, f32[512,2,512]{2,0,1:T(8,128)} %fusion), kind=kOutput, calls=%fused_computation.4 | convolution fusion | flops 3225944064 | bytes 14680064 | tf_op jit(solution)/shard_map/dot_general | solution.py:75
  535.6 95.3 %reduce-scatter.2.cloned.1.call-done = bf16[32,6144]{1,0:T(8,128)(2,1)} async-done(((bf16[512,6144]{1,0:T(8,128)(2,1)}), bf16[32,6144]{1,0:T(8,128)(2,1)}) %reduce-scatter.2.cloned.1.call-update) | async-done | bytes 393232 | tf_op jit(solution)/shard_map/reduce_scatter | solution.py:74
  630.9 1.1 reshape.67
  632.0 20.0 %all_to_all.69 = bf16[8,4,6144]{2,1,0:T(4,128)(2,1)} all-to-all(bf16[8,4,6144]{2,1,0:T(4,128)(2,1)S(1)} %reshape.67), channel_id=1, replica_groups=mesh['dp'=2,'expert'=8,'shard'=16] {'expert'}, dimensions={0} | all-to-all | bytes 786432 | tf_op jit(solution)/shard_map/all_to_all | solution.py:82
  652.0 1.1 reshape.68
  (23 shorter events, 7.0 us)
Async XLA Ops:
  6.5 276.3 %copy-start = (bf16[8,32,6144]{2,1,0:T(8,128)(2,1)S(1)}, bf16[8,32,6144]{2,1,0:T(8,128)(2,1)}, u32[]{:S(2)}) copy-start(bf16[8,32,6144]{2,1,0:T(8,128)(2,1)} %param.10) | copy-start | bytes 9437188
  10.4 23.2 %all-to-all-start = ((bf16[8,4,6144]{2,1,0:T(4,128)(2,1)}), bf16[8,4,6144]{2,1,0:T(4,128)(2,1)S(1)}, u32[]{:S(2)}, u32[]{:S(2)}) async-start(bf16[8,4,6144]{2,1,0:T(4,128)(2,1)} %reshape.62), calls=%async_computation | async-start | bytes 786432 | tf_op jit(solution)/shard_map/all_to_all | solution.py:37
  33.5 96.8 %all-to-all-start.1 = ((bf16[8,2,2,16,6144]{4,3,1,0,2:T(8,128)(2,1)}), bf16[8,2,2,16,6144]{4,3,1,0,2:T(8,128)(2,1)}, u32[]{:S(2)}, u32[]{:S(2)}) async-start(bf16[8,2,2,16,6144]{4,3,1,0,2:T(8,128)(2,1)} %copy.24), calls=%async_computation.1 | async-start | bytes 12582912 | tf_op jit(solution)/shard_map/all_to_all | solution.py:51
  39.8 387.0 %all-gather.3.cloned.1.call-start = ((), (), s32[]{:S(2)}) async-start(), calls=%async_computation.8 | async-start | bytes 6684672 | tf_op jit(solution)/shard_map/all_gather | solution.py:73
  40.8 454.3 %all-gather.5.cloned.1.call-start = ((), (), s32[]{:S(2)}) async-start(), calls=%async_computation.9 | async-start | bytes 18874368 | tf_op jit(solution)/shard_map/all_gather | solution.py:66
  420.4 105.4 %all-to-all-start.5 = ((bf16[2,1,1,1,256,6144]{5,4,3,2,1,0:T(8,128)(2,1)}), bf16[2,1,1,1,256,6144]{5,4,3,2,1,0:T(8,128)(2,1)}, u32[]{:S(2)}, u32[]{:S(2)}) async-start(bf16[2,1,1,1,256,6144]{5,4,3,2,1,0:T(8,128)(2,1)} %pad_maximum_fusion), calls=%async_computation.5 | async-start | bytes 12582912 | tf_op jit(solution)/shard_map/all_to_all | solution.py:68
  426.8 204.1 %reduce-scatter.2.cloned.1.call-start = ((), (), s32[]{:S(2)}) async-start(), calls=%async_computation.10 | async-start | bytes 6684672 | tf_op jit(solution)/shard_map/reduce_scatter | solution.py:74
  525.9 128.2 %copy-start.1 = (bf16[8,32,6144]{2,1,0:T(8,128)(2,1)S(1)}, bf16[8,32,6144]{2,1,0:T(8,128)(2,1)}, u32[]{:S(2)}) copy-start(bf16[8,32,6144]{2,1,0:T(8,128)(2,1)} %param.10) | copy-start | bytes 9437188
Sparse Core Ops, SparseCore 0:
  43.4 90.1 all-gather.2
  282.9 212.0 all-gather.4
  535.7 95.1 reduce-scatter.1
